TPU v7x, 256 devices: a whole 4x4x8 slice. The times are simulated.
256 devices in a mesh: occ: 64 (over x, z, core), aux: 4 (over y).
Axes of the slice: x: 4, y: 4, z: 8, core: 2. Of those that a mesh axis runs over, the one named last changes fastest.
Arguments:
- factors: bfloat16 [128, 256, 1024], P('occ', None, 'aux'), may hold values from -0.8984375 to 0.8984375
- occ_energy: float32 [128], replicated, may hold values from -3 to -0.5
- vir_energy: float32 [256], replicated, may hold values from 0.5 to 3
- i_slot: int32 [2048], P('occ'), may hold values from 0 to 1
- j_slot: int32 [2048], P('occ'), may hold values from 0 to 1
- partner_device: int32 [2048, 1], P('occ'), may hold values from 0 to 63; in each aligned block of 32 rows (0 to 31, 32 to 63, ...) at most 2 rows name the same one
- pair_count: int32 [64], P('occ'), may hold values from 1 to 32, 1843 in all
Outputs:
- gamma: float32 [128, 256, 1024], P('occ', None, 'aux')
- aux_matrix: float32 [1024, 1024], P('aux', 'occ')
Inputs may be any that keep to these rules, and one draw needn't show every extreme that they name: `partner_device`: among the 32 pair slots of one occ index, at most 2 name the same partner device, and some index reaches 2.
All inputs are finite; a program needn't handle non-finite values. No bound on the sum of `pair_count` on one device may be relied on, other than what follows from the above.
Results may differ from a plain program's by a relative error of at most 0.0013.
Values may be sent and summed in bfloat16 or wider, within the bound.
No kernel may reach another device: no remote copies, remote signals or barrier semaphores. Data moves between devices by JAX's collectives and lax.ppermute only.
A program may use at most 128 MiB of HBM per device.

v0:
```python
import jax
import jax.numpy as jnp
from jax import lax
from jax.sharding import PartitionSpec as P


def body(factors, occ_energy, vir_energy, i_slot, j_slot, partner_device, pair_count):
    held, virtuals, columns = factors.shape
    pair_slots = i_slot.shape[0]
    occ_count = lax.axis_size("occ")
    capacity = max(2, (3 * pair_slots // 2 + occ_count - 1) // occ_count)
    slot_total = occ_count * capacity
    device_index = lax.axis_index("occ")
    pair_order = jnp.arange(pair_slots, dtype=jnp.int32)
    living = pair_order < pair_count[0]
    target = partner_device[:, 0]
    earlier = (
        (target[:, None] == target[None, :])
        & living[None, :]
        & (pair_order[None, :] < pair_order[:, None])
    )
    slot_rank = jnp.sum(earlier.astype(jnp.int32), axis=1)
    slot_index = target * capacity + slot_rank
    slot_hit = (slot_index[:, None] == jnp.arange(slot_total, dtype=jnp.int32)[None, :]) & living[
        :, None
    ]
    requests = jnp.sum(jnp.where(slot_hit, j_slot[:, None] + 1, 0), axis=0) - 1
    wanted = lax.all_to_all(requests, "occ", split_axis=0, concat_axis=0, tiled=True)
    wanted_hit = (wanted[:, None] == jnp.arange(held, dtype=jnp.int32)[None, :]).astype(
        jnp.bfloat16
    )
    factor_rows = factors.reshape(held, virtuals * columns)
    far_index = target * held + j_slot
    outgoing = jnp.dot(wanted_hit, factor_rows, preferred_element_type=jnp.float32)
    outgoing = outgoing.astype(jnp.bfloat16).reshape(slot_total, virtuals, columns)
    arrived = lax.all_to_all(outgoing, "occ", split_axis=0, concat_axis=0, tiled=True)
    pick_rows = slot_hit.astype(jnp.bfloat16)
    partner_blocks = jnp.dot(
        pick_rows,
        arrived.reshape(slot_total, virtuals * columns),
        preferred_element_type=jnp.float32,
    )
    partner_blocks = partner_blocks.astype(jnp.bfloat16).reshape(pair_slots, virtuals, columns)
    own_blocks = factors[i_slot]
    orbitals = occ_energy.shape[0]
    table = jnp.arange(orbitals, dtype=jnp.int32)
    own_index = device_index * held + i_slot
    energy_own = jnp.sum(
        jnp.where(own_index[:, None] == table[None, :], occ_energy[None, :], 0.0), axis=1
    )
    energy_far = jnp.sum(
        jnp.where(far_index[:, None] == table[None, :], occ_energy[None, :], 0.0), axis=1
    )
    denominator = (
        vir_energy[None, :, None]
        + vir_energy[None, None, :]
        - energy_own[:, None, None]
        - energy_far[:, None, None]
    )
    partial_value = jnp.einsum(
        "pvq,pwq->pvw", own_blocks, partner_blocks, preferred_element_type=jnp.float32
    )
    summed = lax.psum(partial_value, "aux")
    amplitude = jnp.where(living[:, None, None], summed / denominator, 0.0).astype(jnp.bfloat16)
    local_terms = jnp.einsum(
        "pvw,pwq->pvq", amplitude, partner_blocks, preferred_element_type=jnp.float32
    )
    owner_hit = (i_slot[:, None] == jnp.arange(held, dtype=jnp.int32)[None, :]).astype(jnp.float32)
    gamma_local = jnp.einsum("po,pvq->ovq", owner_hit, local_terms, precision=lax.Precision.HIGHEST)
    return_terms = jnp.einsum(
        "pwv,pwq->pvq", amplitude, own_blocks, preferred_element_type=jnp.float32
    ).astype(jnp.bfloat16)
    placed = jnp.dot(
        slot_hit.astype(jnp.bfloat16).T,
        return_terms.reshape(pair_slots, virtuals * columns),
        preferred_element_type=jnp.float32,
    )
    placed = placed.astype(jnp.bfloat16).reshape(slot_total, virtuals, columns)
    returned = lax.all_to_all(placed, "occ", split_axis=0, concat_axis=0, tiled=True)
    gathered_back = jnp.dot(
        wanted_hit.T,
        returned.reshape(slot_total, virtuals * columns),
        preferred_element_type=jnp.float32,
    )
    gamma = gamma_local + gathered_back.reshape(held, virtuals, columns)
    rounded = gamma.astype(jnp.bfloat16)
    stacked = jnp.stack([rounded, factors])
    gamma_rows = rounded.reshape(held * virtuals, columns)
    factor_flat = factors.reshape(held * virtuals, columns)
    piece = lax.all_gather(stacked, "aux", axis=3, tiled=True)
    width_here = piece.shape[3]
    gamma_piece = piece[0].reshape(held * virtuals, width_here)
    factor_piece = piece[1].reshape(held * virtuals, width_here)
    first = jnp.dot(gamma_rows.T, factor_piece, preferred_element_type=jnp.float32)
    second = jnp.dot(factor_flat.T, gamma_piece, preferred_element_type=jnp.float32)
    terms = first + second
    shared = lax.psum_scatter(terms, "occ", scatter_dimension=1, tiled=True)
    factor_scale = float(orbitals * virtuals) ** (-0.5)
    return (gamma, shared * factor_scale)


def solution(mesh):
    placed = (P("occ", None, "aux"), P(), P(), P("occ"), P("occ"), P("occ", None), P("occ"))
    return jax.shard_map(
        body,
        mesh=mesh,
        in_specs=placed,
        out_specs=(P("occ", None, "aux"), P("aux", "occ")),
        check_vma=False,
    )
```

profile of v0, /device:TPU:8, one launch (start us, length us, event | category | flops | bytes accessed | tf_op | source)
XLA Modules:
  0.0 1268.4 jit_solution(14306813267259421610)
XLA Ops:
  7.8 0.9 convert_reduce_fusion
  8.7 0.7 fusion.20
  9.4 0.7 multiply_add_fusion
  10.1 0.1 select_reduce_fusion.2
  10.2 0.8 sub.28
  11.0 11.9 all-to-all-start
  22.9 1.2 copy.40
  24.1 8.2 all-to-all-done
  32.4 0.5 broadcast.75
  32.9 0.7 reduce.3
  33.6 0.1 eq.95
  33.7 8.1 convolution_convert_fusion.1
  41.8 15.6 %copy.41 = bf16[16,8,256,256]{3,2,1,0:T(8,128)(2,1)} copy(bf16[16,8,256,256]{3,1,2,0:T(8,128)(2,1)} %bitcast.69) | data formatting | bytes 33554432
  57.5 6.0 all-to-all-start.1
  63.5 0.3 all-reduce.2.cloned.1.call-start
  63.8 2.9 gather_fusion
  66.7 361.4 %all-to-all-done.1 = bf16[128,256,256]{2,1,0:T(8,128)(2,1)} async-done(((bf16[128,256,256]{2,1,0:T(8,128)(2,1)}), bf16[128,256,256]{2,1,0:T(8,128)(2,1)}, u32[]{:S(2)}, u32[]{:S(2)}) %all-to-all-start.1) | async-done | bytes 16777248 | tf_op jit(solution)/shard_map/all_to_all | solution.py:36
  428.1 15.8 %copy.42 = bf16[16,8,256,256]{3,1,2,0:T(8,128)(2,1)S(1)} copy(bf16[16,8,256,256]{3,2,1,0:T(8,128)(2,1)} %bitcast.23) | data formatting | bytes 33554432
  443.9 3.9 convolution_convert_fusion.2
  447.8 3.3 copy.43
  451.2 1.9 copy-done.2
  453.1 4.5 fusion.26
  457.7 0.6 copy-done.7
  458.3 0.2 select_reduce_fusion.1
  458.5 0.1 broadcast_add_fusion
  458.6 161.0 %all-reduce.2.cloned.1.call-done = f32[32,256,256]{2,1,0:T(8,128)} async-done(((f32[32,256,256]{2,1,0:T(8,128)}), f32[32,256,256]{2,1,0:T(8,128)}) %all-reduce.2.cloned.1.call-update) | async-done | bytes 8388624 | tf_op jit(solution)/shard_map/psum | solution.py:63
  619.6 5.0 select_convert_fusion
  624.6 1.3 convolution_convert_fusion.3
  625.9 4.4 copy.44
  630.3 12.5 convolution_convert_fusion
  642.9 15.6 %copy.45 = bf16[16,8,256,256]{3,2,1,0:T(8,128)(2,1)} copy(bf16[16,8,256,256]{3,1,2,0:T(8,128)(2,1)} %bitcast.68) | data formatting | bytes 33554432
  658.5 10.7 all-to-all-start.2
  669.2 0.3 copy.53
  669.5 7.9 fusion.27
  677.4 356.4 %all-to-all-done.2 = bf16[128,256,256]{2,1,0:T(8,128)(2,1)} async-done(((bf16[128,256,256]{2,1,0:T(8,128)(2,1)}), bf16[128,256,256]{2,1,0:T(8,128)(2,1)}, u32[]{:S(2)}, u32[]{:S(2)}) %all-to-all-start.2) | async-done | bytes 16777248 | tf_op jit(solution)/shard_map/all_to_all | solution.py:79
  1033.8 23.4 %copy.39 = bf16[128,256,256]{0,2,1:T(8,128)(2,1)} copy(bf16[128,256,256]{2,1,0:T(8,128)(2,1)} %all-to-all-done.2) | data formatting | bytes 33554432 | tf_op jit(solution)/shard_map/reshape | solution.py:82
  1057.3 10.2 fusion
  1067.5 10.6 fusion.25
  1078.0 1.6 pad_maximum_fusion
  1079.7 33.1 %all-gather.2.cloned.1.call-done = bf16[2,2,256,1024]{3,1,2,0:T(2,128)(2,1)} async-done(((bf16[2,2,256,256]{3,1,2,0:T(2,128)(2,1)}), bf16[2,2,256,1024]{3,1,2,0:T(2,128)(2,1)}) %all-gather.2.cloned.1.call-update) | async-done | bytes 2097168 | tf_op jit(solution)/shard_map/all_gather | solution.py:90
  1112.8 2.9 fusion.24
  1115.7 0.3 copy.35
  1116.0 0.3 copy.36
  1116.2 0.6 fusion.28
  1116.8 1.4 fusion.4
  1118.3 0.8 copy.37
  1119.1 141.2 %reduce-scatter.2.cloned.1.call-done = f32[256,16]{0,1:T(8,128)} async-done(((f32[256,1024]{0,1:T(8,128)}), f32[256,16]{0,1:T(8,128)}) %reduce-scatter.2.cloned.1.call-update) | async-done | bytes 16400 | tf_op jit(solution)/shard_map/reduce_scatter | solution.py:97
  1260.3 1.3 broadcast_multiply_fusion
  (23 shorter events, 0.2 us)
Async XLA Ops:
  11.0 21.4 %all-to-all-start = ((s32[64,2,1]{1,2,0:T(1,128)}), s32[64,2,1]{1,2,0:T(1,128)S(1)}, u32[]{:S(2)}, u32[]{:S(2)}) async-start(s32[64,2,1]{1,2,0:T(1,128)} %bitcast.5), calls=%async_computation | async-start | bytes 65536 | tf_op jit(solution)/shard_map/all_to_all | solution.py:28
  57.5 6.4 copy-start
  57.5 370.7 %all-to-all-start.1 = ((bf16[128,256,256]{2,1,0:T(8,128)(2,1)}), bf16[128,256,256]{2,1,0:T(8,128)(2,1)}, u32[]{:S(2)}, u32[]{:S(2)}) async-start(bf16[128,256,256]{2,1,0:T(8,128)(2,1)} %bitcast.66), calls=%async_computation.1 | async-start | bytes 33554432 | tf_op jit(solution)/shard_map/all_to_all | solution.py:36
  63.5 556.1 %all-reduce.2.cloned.1.call-start = ((), (), s32[]{:S(2)}) async-start(), calls=%async_computation.4 | async-start | bytes 16777216 | tf_op jit(solution)/shard_map/psum | solution.py:63
  447.8 5.3 copy-start.3
  451.2 1.9 copy-start.2
  457.6 0.7 copy-start.7
  457.6 0.8 copy-start.5
  619.6 5.0 copy-start.4
  624.6 5.7 copy-start.1
  658.5 375.4 %all-to-all-start.2 = ((bf16[128,256,256]{2,1,0:T(8,128)(2,1)}), bf16[128,256,256]{2,1,0:T(8,128)(2,1)}, u32[]{:S(2)}, u32[]{:S(2)}) async-start(bf16[128,256,256]{2,1,0:T(8,128)(2,1)} %bitcast.67), calls=%async_computation.2 | async-start | bytes 33554432 | tf_op jit(solution)/shard_map/all_to_all | solution.py:79
  669.2 443.6 %all-gather.2.cloned.1.call-start = ((), (), s32[]{:S(2)}) async-start(), calls=%async_computation.5 | async-start | bytes 2621440 | tf_op jit(solution)/shard_map/all_gather | solution.py:90
  1057.3 10.2 copy-start.6
  1079.6 180.7 %reduce-scatter.2.cloned.1.call-start = ((), (), s32[]{:S(2)}) async-start(), calls=%async_computation.6 | async-start | bytes 1064960 | tf_op jit(solution)/shard_map/reduce_scatter | solution.py:97
Sparse Core Ops, SparseCore 0:
  457.8 161.7 all-reduce.1
  1079.7 33.0 all-gather.1
  1118.4 141.9 reduce-scatter.1
where the time goes:
time: 1270 us
  waiting for transfers between devices  1060 us (83%)
  local copies, waits for them, and re-layouts  90.8 us (7%)
  matrix products  61 us (5%)
  starting transfers between devices  29.1 us (2%)
  between operations  14.8 us (1%)
    all_to_all x1, waiting for transfers between devices, body(): lax.all_to_all(outgoing, 'occ', split_axis=0, concat_axis=0, tiled=True)  361 us
    all_to_all x1, waiting for transfers between devices, body(): lax.all_to_all(placed, 'occ', split_axis=0, concat_axis=0, tiled=True)  356 us
    psum x1, waiting for transfers between devices, body(): summed = lax.psum(partial_value, 'aux')  161 us
    reduce_scatter x1, waiting for transfers between devices, body(): shared = lax.psum_scatter(terms, 'occ', scatter_dimension=1, tiled=True)  141 us
    unnamed x24, local copies, waits for them, and re-layouts  59.7 us
    all_gather x1, waiting for transfers between devices, body(): piece = lax.all_gather(stacked, 'aux', axis=3, tiled=True)  33.1 us
  transfers between devices with their start and end apart: 6, of which 6 were waited for; matrix products, arithmetic and copies ran while one was open for 1% of the time, Pallas kernels for 0%

commit v1 on v0

v1 whole, which is shorter than its diff:
```python
import functools

import jax
import jax.numpy as jnp
from jax import lax
from jax.experimental import pallas as pl
from jax.experimental.pallas import tpu as pltpu
from jax.sharding import PartitionSpec as P


def pair_block(virtuals, own_ref, far_ref, row_ref, col_ref, weight_ref, out_ref):
    @pl.when(pl.program_id(0) == 0)
    def _():
        out_ref[...] = jnp.zeros_like(out_ref)

    far = far_ref[...]
    for k in range(own_ref.shape[0] // virtuals):
        rows = pl.ds(k * virtuals, virtuals)
        meet = lax.dot_general(
            own_ref[rows, :], far, (((1,), (1,)), ((), ())), preferred_element_type=jnp.float32
        )
        gap = row_ref[rows, :] + col_ref[...]
        amplitude = (meet / gap).astype(jnp.bfloat16) * weight_ref[k : k + 1, :].astype(jnp.bfloat16)
        out_ref[rows, :] += jnp.dot(amplitude, far, preferred_element_type=jnp.float32)


def contract(own, far, row, col, weight, virtuals, tile):
    rows, width = own.shape
    far_rows = far.shape[0]
    whole = lambda t: (0, 0)
    return pl.pallas_call(
        functools.partial(pair_block, virtuals),
        out_shape=jax.ShapeDtypeStruct((rows, width), jnp.float32),
        grid=(far_rows // tile,),
        in_specs=[
            pl.BlockSpec((rows, width), whole),
            pl.BlockSpec((tile, width), lambda t: (t, 0)),
            pl.BlockSpec((rows, 1), whole),
            pl.BlockSpec((1, tile), lambda t: (0, t)),
            pl.BlockSpec((weight.shape[0], tile), lambda t: (0, t)),
        ],
        out_specs=pl.BlockSpec((rows, width), whole),
        cost_estimate=pl.CostEstimate(
            flops=4 * rows * far_rows * width, bytes_accessed=2 * far_rows * width, transcendentals=0
        ),
        name="pair_block",
    )(own, far, row, col, weight)


def body(factors, occ_energy, vir_energy, i_slot, j_slot, partner_device, pair_count):
    held, virtuals, columns = factors.shape
    pair_slots = i_slot.shape[0]
    occ_count = lax.axis_size("occ")
    aux_count = lax.axis_size("aux")
    orbitals = occ_energy.shape[0]
    me, part = lax.axis_index("occ"), lax.axis_index("aux")
    rows = held * virtuals
    share = rows // aux_count
    parts_per_orbital = virtuals // share
    slot_of_part = part // parts_per_orbital
    first_virtual = (part % parts_per_orbital) * share

    living = jnp.arange(pair_slots, dtype=jnp.int32) < pair_count[0]
    far_index = partner_device[:, 0] * held + j_slot
    own_hot = (i_slot[:, None] == jnp.arange(held, dtype=jnp.int32)[None, :]) & living[:, None]
    far_hot = far_index[:, None] == jnp.arange(orbitals, dtype=jnp.int32)[None, :]
    counts = jnp.sum(
        (own_hot[:, :, None] & far_hot[:, None, :]).astype(jnp.int32), axis=0
    )
    sent = counts.reshape(held, occ_count, held).transpose(1, 0, 2)
    back = lax.all_to_all(sent, "occ", split_axis=0, concat_axis=0, tiled=True)
    weight = counts + back.transpose(2, 0, 1).reshape(held, orbitals)
    weight = lax.dynamic_index_in_dim(
        weight.reshape(held, occ_count, held), slot_of_part, axis=2, keepdims=False
    ).astype(jnp.float32)
    weight = jnp.broadcast_to(weight[:, :, None], (held, occ_count, share)).reshape(held, -1)

    own_energy = lax.dynamic_slice(occ_energy, (me * held,), (held,))
    row = (vir_energy[None, :] - own_energy[:, None]).reshape(rows, 1)
    far_energy = lax.dynamic_index_in_dim(
        occ_energy.reshape(occ_count, held), slot_of_part, axis=1, keepdims=False
    )
    far_virtual = lax.dynamic_slice(vir_energy, (first_virtual,), (share,))
    col = (far_virtual[None, :] - far_energy[:, None]).reshape(1, -1)

    own = lax.all_gather(factors, "aux", axis=2, tiled=True).reshape(rows, -1)
    mine = lax.dynamic_slice(own, (part * share, 0), (share, own.shape[1]))
    far = lax.all_gather(mine, "occ", axis=0, tiled=True)

    partial = contract(own, far, row, col, weight, virtuals, 4 * share)
    gamma = lax.psum_scatter(partial, "aux", scatter_dimension=1, tiled=True)
    rounded = gamma.astype(jnp.bfloat16)
    terms = lax.dot_general(
        own, rounded, (((0,), (0,)), ((), ())), preferred_element_type=jnp.float32
    )
    spread = lax.all_to_all(terms, "occ", split_axis=0, concat_axis=0, tiled=True)
    total = jnp.sum(spread.reshape(occ_count, -1, columns), axis=0)
    scale = 2.0 * float(orbitals * virtuals) ** (-0.5)
    return gamma.reshape(held, virtuals, columns), total.T * scale


def solution(mesh):
    placed = (P("occ", None, "aux"), P(), P(), P("occ"), P("occ"), P("occ", None), P("occ"))
    return jax.shard_map(
        body,
        mesh=mesh,
        in_specs=placed,
        out_specs=(P("occ", None, "aux"), P("aux", "occ")),
        check_vma=False,
    )
```

time: 1270 us -> 250 us (0.20)
  waiting for transfers between devices: 1060 us -> 144 us
  local copies, waits for them, and re-layouts: 90.8 us -> 7.34 us
  matrix products: 61 us -> 1.51 us
  blocking collectives: 0 us -> 38.4 us
  Pallas kernels: 0 us -> 26.9 us
  starting transfers between devices: 29.1 us -> 10.6 us
    all_to_all x3 -> x1, waiting for transfers between devices: 726 us -> 4.86 us  [body(): back = lax.all_to_all(sent, 'occ', split_axis=0, concat_axis=0, tiled=True)]
    psum x1 -> x0, waiting for transfers between devices: 161 us -> none  [body(): summed = lax.psum(partial_value, 'aux')]
    reduce_scatter x1, waiting for transfers between devices: 141 us -> 28.2 us  [body(): gamma = lax.psum_scatter(partial, 'aux', scatter_dimension=1, tiled=True)]
    all_gather x1 -> x2, waiting for transfers between devices: 33.1 us -> 110 us  [the longest x1 78 us: body(): far = lax.all_gather(mine, 'occ', axis=0, tiled=True)]
    dot_general x10 -> x1, matrix products: 61 us -> 1.51 us  [body(): lax.dot_general(own, rounded, (((0,), (0,)), ((), ())), preferred_element...]
    unnamed x24 -> x6, local copies, waits for them, and re-layouts: 59.7 us -> 1.65 us
    all_to_all x0 -> x1, blocking collectives: none -> 38.4 us  [body(): lax.all_to_all(terms, 'occ', split_axis=0, concat_axis=0, tiled=True)]
    pallas_call x0 -> x1, Pallas kernels: none -> 26.9 us  [contract(): pl.pallas_call(functools.partial(pair_block, virtuals), out_shape=jax.Sha...]
  transfers between devices with their start and end apart: 6 -> 4, of which waited for: 6 -> 4; matrix products, arithmetic and copies ran while one was open for 1% -> 3% of each run, Pallas kernels for 0% -> 0%
where the time goes in v1:
time: 250 us; the launch traced here: 247 us
  waiting for transfers between devices  144 us (58%)
  blocking collectives  38.4 us (15%)
  Pallas kernels  26.9 us (11%)
  between operations  14.5 us (6%)
  starting transfers between devices  10.6 us (4%)
  local copies, waits for them, and re-layouts  7.34 us (3%)
  other arithmetic  3.84 us (2%)
    all_gather x1, waiting for transfers between devices, body(): far = lax.all_gather(mine, 'occ', axis=0, tiled=True)  78 us
    all_to_all x1, blocking collectives, body(): lax.all_to_all(terms, 'occ', split_axis=0, concat_axis=0, tiled=True)  38.4 us
    all_gather x1, waiting for transfers between devices, body(): own = lax.all_gather(factors, 'aux', axis=2, tiled=True).reshape(rows, -1)  32 us
    reduce_scatter x1, waiting for transfers between devices, body(): gamma = lax.psum_scatter(partial, 'aux', scatter_dimension=1, tiled=True)  28.2 us
    pallas_call x1, Pallas kernels, contract(): pl.pallas_call(functools.partial(pair_block, virtuals), out_shape=jax.Sha...  26.9 us
    all_to_all x1, starting transfers between devices, body(): back = lax.all_to_all(sent, 'occ', split_axis=0, concat_axis=0, tiled=True)  10.4 us
  transfers between devices with their start and end apart: 4, of which 4 were waited for; matrix products, arithmetic and copies ran while one was open for 3% of the time, Pallas kernels for 0%

profile of v1, /device:TPU:8, one launch (start us, length us, event | category | flops | bytes accessed | tf_op | source)
XLA Modules:
  0.0 246.8 jit_solution(8208366226813759148)
XLA Ops:
  7.2 0.0 all-gather.3.cloned.1.call-start
  7.2 0.7 all-gather.3.cloned.1.call-update
  7.9 0.0 all-gather.5.cloned.1.call-start
  7.9 32.0 %all-gather.3.cloned.1.call-done = bf16[2,256,1024]{2,1,0:T(8,128)(2,1)} async-done(((bf16[2,256,256]{2,1,0:T(8,128)(2,1)}), bf16[2,256,1024]{2,1,0:T(8,128)(2,1)}) %all-gather.3.cloned.1.call-update) | async-done | bytes 1048592 | tf_op jit(solution)/shard_map/all_gather | solution.py:86
  40.0 1.7 constant_dynamic-slice_fusion
  41.7 0.0 all-gather.5.cloned.1.call-update
  42.3 0.7 compare_and_fusion
  43.0 0.7 bitcast_add_fusion
  43.7 0.1 iota_compare_fusion
  43.8 0.1 convert_reduce_fusion
  43.9 0.1 reduce_sum.21
  44.0 1.1 copy.20
  45.1 10.4 %all-to-all-start = ((s32[64,2,2]{1,2,0:T(2,128)}), s32[64,2,2]{1,2,0:T(2,128)S(1)}, u32[]{:S(2)}, u32[]{:S(2)}) async-start(s32[64,2,2]{1,2,0:T(2,128)} %copy.20), calls=%async_computation | async-start | bytes 131072 | tf_op jit(solution)/shard_map/all_to_all | solution.py:71
  55.5 0.0 reduce-scatter.2.cloned.1.call-start
  55.6 0.8 reshape.133
  56.4 0.7 dynamic_slice.18
  57.2 0.8 dynamic_slice.19
  57.9 0.2 dynamic-slice_reduce_fusion
  58.1 0.7 broadcast_subtract_fusion
  58.8 0.7 subtract_bitcast_fusion
  59.5 0.9 copy.25
  60.4 4.9 %all-to-all-done = s32[64,2,2]{1,2,0:T(2,128)S(1)} async-done(((s32[64,2,2]{1,2,0:T(2,128)}), s32[64,2,2]{1,2,0:T(2,128)S(1)}, u32[]{:S(2)}, u32[]{:S(2)}) %all-to-all-start) | async-done | bytes 1056 | tf_op jit(solution)/shard_map/all_to_all | solution.py:71
  65.3 0.2 fusion.2
  65.5 0.1 broadcast_bitcast_fusion
  65.5 0.7 copy.29
  66.2 78.0 %all-gather.5.cloned.1.call-done.far_ref = bf16[8192,1024]{1,0:T(8,128)(2,1)} async-done(((bf16[128,1024]{1,0:T(8,128)(2,1)}), bf16[8192,1024]{1,0:T(8,128)(2,1)}) %all-gather.5.cloned.1.call-update) | async-done | bytes 16777232 | tf_op jit(solution)/shard_map/all_gather | solution.py:88
  144.2 0.0 copy-start
  144.2 26.9 %pair_block.1 = f32[512,1024]{1,0:T(8,128)} custom-call(bf16[512,1024]{1,0:T(8,128)(2,1)} %bitcast.29, bf16[8192,1024]{1,0:T(8,128)(2,1)} %all-gather.5.cloned.1.call-done.far_ref, f32[512,1]{1,0:T(8,128)} %bitcast.33, f32[1,8192]{1,0:T(1,128)} %bitcast.36, f32[2,8192]{1,0:T(2,128)} %bitcast.35), custom_call_target="tpu_custom_call" | custom-call | flops 17179869184 | bytes 16777216 | tf_op jit(solution)/shard_map/pair_block/pallas_call | solution.py:31
  171.1 0.0 reduce-scatter.2.cloned.1.call-update
  171.1 28.2 %reduce-scatter.2.cloned.1.call-done = f32[512,256]{1,0:T(8,128)} async-done(((f32[512,1024]{1,0:T(8,128)}), f32[512,256]{1,0:T(8,128)}) %reduce-scatter.2.cloned.1.call-update) | async-done | bytes 524304 | tf_op jit(solution)/shard_map/reduce_scatter | solution.py:91
  199.3 0.0 copy-done
  199.3 1.5 convolution_bitcast_fusion
  200.8 0.3 copy.23
  201.2 38.4 %all_to_all.14 = f32[64,16,256]{2,1,0:T(8,128)S(1)} all-to-all(f32[64,16,256]{2,1,0:T(8,128)S(1)} %bitcast.27), channel_id=1, replica_groups=mesh['occ'=64,'aux'=4] {'occ'}, dimensions={0} | all-to-all | bytes 2097152 | tf_op jit(solution)/shard_map/all_to_all | solution.py:96
  239.6 0.1 reduce_sum.22
  239.7 0.6 multiply_bitcast_fusion
  (3 shorter events, 0.0 us)
Async XLA Ops:
  7.2 32.8 %all-gather.3.cloned.1.call-start = ((), (), s32[]{:S(2)}) async-start(), calls=%async_computation.3 | async-start | bytes 1310720 | tf_op jit(solution)/shard_map/all_gather | solution.py:86
  7.9 136.3 %all-gather.5.cloned.1.call-start = ((), (), s32[]{:S(2)}) async-start(), calls=%async_computation.4 | async-start | bytes 17039360 | tf_op jit(solution)/shard_map/all_gather | solution.py:88
  45.1 20.2 %all-to-all-start = ((s32[64,2,2]{1,2,0:T(2,128)}), s32[64,2,2]{1,2,0:T(2,128)S(1)}, u32[]{:S(2)}, u32[]{:S(2)}) async-start(s32[64,2,2]{1,2,0:T(2,128)} %copy.20), calls=%async_computation | async-start | bytes 131072 | tf_op jit(solution)/shard_map/all_to_all | solution.py:71
  55.5 143.8 %reduce-scatter.2.cloned.1.call-start = ((), (), s32[]{:S(2)}) async-start(), calls=%async_computation.5 | async-start | bytes 2621440 | tf_op jit(solution)/shard_map/reduce_scatter | solution.py:91
  144.2 55.2 %copy-start = (bf16[2,256,1024]{2,1,0:T(8,128)(2,1)S(1)}, bf16[2,256,1024]{2,1,0:T(8,128)(2,1)}, u32[]{:S(2)}) copy-start(bf16[2,256,1024]{2,1,0:T(8,128)(2,1)} %all-gather.3.cloned.1.call-done) | copy-start | bytes 3145732
Sparse Core Ops, SparseCore 0:
  9.8 30.1 all-gather.2
  43.3 100.7 all-gather.4
  171.3 28.0 reduce-scatter.1
